TPU v7x, 512 devices: a whole 4x4x16 slice. The times are simulated.
512 devices in a mesh: row: 128 (over y, z, core), col: 4 (over x).
Axes of the slice: x: 4, y: 4, z: 16, core: 2. Of those that a mesh axis runs over, the one named last changes fastest.
Arguments:
- residual: float32 [65536, 128], P('row'), may hold values from -6 to 6
- solution: float32 [65536, 128], P('row'), may hold values from -6 to 6
- near_field_blocks: float32 [256, 4, 256, 256], P('row', 'col'), may hold values from -0.09375 to 0.09375
- near_cols: int32 [256, 4], P('row', 'col'), may hold values from 0 to 255, as said below
- couplings: float32 [256, 64, 16, 16], P('row', 'col'), may hold values from -0.1875 to 0.1875
- far_cols: int32 [256, 64], P('row', 'col'), may hold values from 0 to 255, as said below
- far_count: int32 [256], P('row'), may hold values from 16 to 64, as said below
- col_basis: float32 [256, 16, 256], P('row'), may hold values from -0.375 to 0.375
- row_basis: float32 [256, 16, 256], P('row'), may hold values from -0.75 to 0.75
Outputs:
- solution_next: float32 [65536, 128], P('row')
- hessenberg: float32 [5, 4, 128], replicated
Inputs may be any that keep to these rules, and one draw needn't show every extreme that they name: near_cols[i, 0] = i; the other entries of row cluster i are i + t for distinct nonzero t with |t| <= 2, clipped to 0 .. 255. far_cols[i, p] differs from i by more than 2, counted around the ends of the cluster range. Slots p >= far_count[i] of row cluster i are unused; some row cluster uses all 64 slots.
All inputs are finite; a program needn't handle non-finite values.
Results may differ from a plain program's by a relative error of at most 0.0001.
Values sent between devices are 32-bit elements; how exact they have to be, the bound alone decides.
A program may use at most 64 MiB of HBM per device.

v0:
```python
import jax
import jax.numpy as jnp
from jax import lax
from jax.sharding import PartitionSpec as P

LEAF_UNKNOWNS = 256
CL_DEV = 2
REACH = 2
SB = 4


HIGH = lax.Precision.HIGHEST
SHIFT = 1.0


def with_halo(value, sides, width):
    for axis, dim in sides:
        peers, length = (lax.axis_size(axis), value.shape[dim])
        up = [(i, (i + 1) % peers) for i in range(peers - 1)]
        down = [(j, i) for i, j in up]
        last = lax.slice_in_dim(value, length - width, length, axis=dim)
        first = lax.slice_in_dim(value, 0, width, axis=dim)
        before = lax.ppermute(last, axis, up)
        after = lax.ppermute(first, axis, down)
        value = jnp.concatenate([before, value, after], axis=dim)
    return value


def cholesky_upper(entries, order_n):
    zero_entry = jnp.zeros_like(entries[0][0])
    upper_r = []
    for row_idx in range(order_n):
        upper_r.append([zero_entry] * order_n)
    for row_idx in range(order_n):
        running = entries[row_idx][row_idx]
        for earlier in range(row_idx):
            running = running - upper_r[earlier][row_idx] * upper_r[earlier][row_idx]
        pivot_val = jnp.sqrt(running)
        upper_r[row_idx][row_idx] = pivot_val
        for col_idx in range(row_idx + 1, order_n):
            entry_val = entries[row_idx][col_idx]
            for earlier in range(row_idx):
                entry_val = entry_val - upper_r[earlier][row_idx] * upper_r[earlier][col_idx]
            upper_r[row_idx][col_idx] = entry_val / pivot_val
    return upper_r


def small_update(gram_sum, scale_factor, depth_n):
    order_n = depth_n + 1
    entries = [
        [gram_sum[row_idx, col_idx] for col_idx in range(order_n)] for row_idx in range(order_n)
    ]
    upper_r = cholesky_upper(entries, order_n)
    shifted = [
        [
            SHIFT * upper_r[row_idx][col_idx] + upper_r[row_idx][col_idx + 1]
            for col_idx in range(depth_n)
        ]
        for row_idx in range(order_n)
    ]
    hessen = []
    for row_idx in range(order_n):
        row_vals = []
        for col_idx in range(depth_n):
            entry_val = shifted[row_idx][col_idx]
            for earlier in range(col_idx):
                entry_val = entry_val - row_vals[earlier] * upper_r[earlier][col_idx]
            row_vals.append(entry_val / upper_r[col_idx][col_idx])
        hessen.append(row_vals)
    normal = []
    for row_idx in range(depth_n):
        row_vals = []
        for col_idx in range(depth_n):
            entry_val = hessen[0][row_idx] * hessen[0][col_idx]
            for inner in range(1, order_n):
                entry_val = entry_val + hessen[inner][row_idx] * hessen[inner][col_idx]
            row_vals.append(entry_val)
        normal.append(row_vals)
    target = [scale_factor * upper_r[0][0] * hessen[0][col_idx] for col_idx in range(depth_n)]
    factor = cholesky_upper(normal, depth_n)
    forward = []
    for row_idx in range(depth_n):
        entry_val = target[row_idx]
        for earlier in range(row_idx):
            entry_val = entry_val - factor[earlier][row_idx] * forward[earlier]
        forward.append(entry_val / factor[row_idx][row_idx])
    solved = [None] * depth_n
    for row_idx in range(depth_n - 1, -1, -1):
        entry_val = forward[row_idx]
        for later in range(row_idx + 1, depth_n):
            entry_val = entry_val - factor[row_idx][later] * solved[later]
        solved[row_idx] = entry_val / factor[row_idx][row_idx]
    weights = [None] * depth_n
    for row_idx in range(depth_n - 1, -1, -1):
        entry_val = solved[row_idx]
        for later in range(row_idx + 1, depth_n):
            entry_val = entry_val - upper_r[row_idx][later] * weights[later]
        weights[row_idx] = entry_val / upper_r[row_idx][row_idx]
    hess_array = jnp.stack([jnp.stack(hessen[row_idx], 0) for row_idx in range(order_n)], 0)
    return (hess_array, weights)


def local(
    residual,
    solution,
    near_field_blocks,
    near_cols,
    couplings,
    far_cols,
    far_count,
    col_basis,
    row_basis,
):
    first_cluster = lax.axis_index("row") * CL_DEV
    blocks, couple = (near_field_blocks, couplings)
    near_idx, far_idx = (near_cols, far_cols)
    positions = lax.axis_index("col") * couplings.shape[1] + jnp.arange(
        couplings.shape[1], dtype=jnp.int32
    )
    live_mask = (positions[None, :] < far_count[:, None]).astype(jnp.float32)
    weighted = couple * live_mask[:, :, None, None]
    local_near = near_idx - (first_cluster - REACH)
    scale_factor = jnp.ones((residual.shape[1],), jnp.float32)
    current = residual
    basis_list = [current]
    for step_k in range(SB):
        width_r = current.shape[1]
        extended = with_halo(current, (("row", 0),), REACH * LEAF_UNKNOWNS)
        panels = extended.reshape(CL_DEV + 2 * REACH, LEAF_UNKNOWNS, width_r)
        picked = jnp.take(panels, local_near, axis=0)
        near_part = jnp.einsum("csab,csbr->car", blocks, picked, precision=HIGH)
        own_panels = current.reshape(CL_DEV, LEAF_UNKNOWNS, width_r)
        coeffs = jnp.einsum("ckb,cbr->ckr", col_basis, own_panels, precision=HIGH)
        table = lax.all_gather(coeffs, "row", axis=0, tiled=True)
        fetched = jnp.take(table, far_idx, axis=0)
        summed = jnp.einsum("cfkl,cflr->ckr", weighted, fetched, precision=HIGH)
        far_part = jnp.einsum("ckb,ckr->cbr", row_basis, summed, precision=HIGH)
        partial_value = (near_part + far_part).reshape(CL_DEV * LEAF_UNKNOWNS, width_r)
        current = lax.psum(partial_value, "col")
        basis_list.append(current)
    stacked = jnp.stack(basis_list, 0)
    local_gram = jnp.einsum("anr,bnr->abr", stacked, stacked, precision=HIGH)
    gram_sum = lax.psum(local_gram, "row")
    hessenberg, weights = small_update(gram_sum, scale_factor, SB)
    new_sol = solution
    for step_k in range(SB):
        new_sol = new_sol + weights[step_k][None, :] * basis_list[step_k]
    return (new_sol, hessenberg)


def solution(mesh):
    placed = (
        P("row", None),
        P("row", None),
        P("row", "col", None, None),
        P("row", "col"),
        P("row", "col", None, None),
        P("row", "col"),
        P("row"),
        P("row", None, None),
        P("row", None, None),
    )
    return jax.shard_map(
        local, mesh=mesh, in_specs=placed, out_specs=(P("row", None), P()), check_vma=False
    )
```

profile of v0, /device:TPU:1, one launch (start us, length us, event | category | flops | bytes accessed | tf_op | source)
XLA Modules:
  0.0 1342.5 jit_solution(8567163214037070050)
XLA Ops:
  7.2 1.9 fusion.85
  9.2 4.9 collective-permute-start
  14.1 5.1 collective-permute-start.1
  22.0 1.0 pad_maximum_fusion
  23.6 134.6 %all-gather.5.cloned.1.call-done = f32[256,16,128]{2,1,0:T(8,128)} async-done(((f32[2,16,128]{2,1,0:T(8,128)}), f32[256,16,128]{2,1,0:T(8,128)}) %all-gather.5.cloned.1.call-update) | async-done | bytes 2097168 | tf_op jit(solution)/shard_map/all_gather | solution.py:134
  158.2 2.2 gather_fusion.1
  162.6 0.8 copy.47
  163.5 51.1 %all-reduce.5.cloned.1.call-done = f32[512,128]{0,1:T(8,128)} async-done(((f32[512,128]{0,1:T(8,128)}), f32[512,128]{0,1:T(8,128)}) %all-reduce.5.cloned.1.call-update) | async-done | bytes 262160 | tf_op jit(solution)/shard_map/psum | solution.py:139
  214.6 1.1 copy.50
  215.7 0.9 convolution_bitcast_fusion.3
  216.6 5.9 collective-permute-start.2
  222.5 1.9 collective-permute-start.3
  224.4 1.7 collective-permute-done.2
  226.1 4.3 collective-permute-done.3
  230.4 1.0 pad_maximum_fusion.1
  232.2 129.9 %all-gather.7.cloned.1.call-done = f32[256,16,128]{2,1,0:T(8,128)} async-done(((f32[2,16,128]{2,1,0:T(8,128)}), f32[256,16,128]{2,1,0:T(8,128)}) %all-gather.7.cloned.1.call-update) | async-done | bytes 2097168 | tf_op jit(solution)/shard_map/all_gather | solution.py:134
  362.2 2.2 gather_fusion.3
  366.5 0.8 copy.52
  367.4 51.1 %all-reduce.7.cloned.1.call-done = f32[512,128]{0,1:T(8,128)} async-done(((f32[512,128]{0,1:T(8,128)}), f32[512,128]{0,1:T(8,128)}) %all-reduce.7.cloned.1.call-update) | async-done | bytes 262160 | tf_op jit(solution)/shard_map/psum | solution.py:139
  418.5 1.1 copy.55
  419.6 0.9 convolution_bitcast_fusion.2
  420.5 5.9 collective-permute-start.4
  426.4 1.9 collective-permute-start.5
  428.3 1.7 collective-permute-done.4
  430.0 4.3 collective-permute-done.5
  434.3 1.0 pad_maximum_fusion.2
  436.1 129.8 %all-gather.9.cloned.1.call-done = f32[256,16,128]{2,1,0:T(8,128)} async-done(((f32[2,16,128]{2,1,0:T(8,128)}), f32[256,16,128]{2,1,0:T(8,128)}) %all-gather.9.cloned.1.call-update) | async-done | bytes 2097168 | tf_op jit(solution)/shard_map/all_gather | solution.py:134
  565.9 2.2 gather_fusion.5
  570.2 0.8 copy.57
  571.2 51.1 %all-reduce.9.cloned.1.call-done = f32[512,128]{0,1:T(8,128)} async-done(((f32[512,128]{0,1:T(8,128)}), f32[512,128]{0,1:T(8,128)}) %all-reduce.9.cloned.1.call-update) | async-done | bytes 262160 | tf_op jit(solution)/shard_map/psum | solution.py:139
  622.3 1.1 copy.60
  623.3 0.9 convolution_bitcast_fusion.1
  624.3 5.9 collective-permute-start.6
  630.2 2.1 collective-permute-start.7
  632.3 1.5 collective-permute-done.6
  633.8 4.3 collective-permute-done.7
  638.1 1.0 pad_maximum_fusion.3
  639.9 129.9 %all-gather.11.cloned.1.call-done = f32[256,16,128]{2,1,0:T(8,128)} async-done(((f32[2,16,128]{2,1,0:T(8,128)}), f32[256,16,128]{2,1,0:T(8,128)}) %all-gather.11.cloned.1.call-update) | async-done | bytes 2097168 | tf_op jit(solution)/shard_map/all_gather | solution.py:134
  769.9 2.2 gather_fusion.7
  775.9 0.8 copy.76
  777.6 1.0 copy.63
  778.6 1.0 copy.64
  779.6 0.9 stack.74
  780.5 45.7 %all-reduce.11.cloned.1.call-done = f32[1,512,128]{1,0,2:T(1,128)} async-done(((f32[1,512,128]{1,0,2:T(1,128)}), f32[1,512,128]{1,0,2:T(1,128)}) %all-reduce.11.cloned.1.call-update) | async-done | bytes 262160 | tf_op jit(solution)/shard_map/psum | solution.py:139
  826.2 4.6 stack.76
  830.7 3.7 convolution_bitcast_fusion
  834.4 492.2 %psum.39 = f32[5,5,128]{0,1,2:T(8,128)S(1)} all-reduce(f32[5,5,128]{0,1,2:T(8,128)} %convolution_bitcast_fusion), channel_id=1, replica_groups=mesh['row'=128,'col'=4] {'row'}, use_global_device_ids=true, to_apply=%region_4.7 | all-reduce | flops 3200 | bytes 25600 | tf_op jit(solution)/shard_map/psum | solution.py:143
  1326.6 6.9 multiply_reduce_fusion
  (91 shorter events, 19.3 us)
Async XLA Ops:
  7.2 154.5 %copy-start = (f32[2,1,256,256]{3,2,1,0:T(8,128)S(1)}, f32[2,1,256,256]{3,2,1,0:T(8,128)}, u32[]{:S(2)}) copy-start(f32[2,1,256,256]{3,2,1,0:T(8,128)} %param.15) | copy-start | bytes 1572868
  7.2 153.2 %copy-start.1 = (f32[2,16,16,16]{3,2,1,0:T(8,128)S(1)}, f32[2,16,16,16]{3,2,1,0:T(8,128)}, u32[]{:S(2)}) copy-start(f32[2,16,16,16]{3,2,1,0:T(8,128)} %param.17) | copy-start | bytes 98308
  7.2 154.0 %copy-start.9 = (f32[2,16,256]{2,1,0:T(8,128)S(1)}, f32[2,16,256]{2,1,0:T(8,128)}, u32[]{:S(2)}) copy-start(f32[2,16,256]{2,1,0:T(8,128)} %param.21) | copy-start | bytes 98308
  7.2 151.0 %all-gather.5.cloned.1.call-start = ((), (), s32[]{:S(2)}) async-start(), calls=%async_computation | async-start | bytes 2113536 | tf_op jit(solution)/shard_map/all_gather | solution.py:134
  9.2 205.4 %all-reduce.5.cloned.1.call-start = ((), (), s32[]{:S(2)}) async-start(), calls=%async_computation.1 | async-start | bytes 524288 | tf_op jit(solution)/shard_map/psum | solution.py:139
  9.2 12.3 collective-permute-start
  14.1 7.9 collective-permute-start.1
  160.4 55.3 %copy-start.8 = (f32[2,16,256]{2,1,0:T(8,128)S(1)}, f32[2,16,256]{2,1,0:T(8,128)}, u32[]{:S(2)}) copy-start(f32[2,16,256]{2,1,0:T(8,128)} %param.20) | copy-start | bytes 98308
  163.4 198.8 %all-gather.7.cloned.1.call-start = ((), (), s32[]{:S(2)}) async-start(), calls=%async_computation.2 | async-start | bytes 2113536 | tf_op jit(solution)/shard_map/all_gather | solution.py:134
  216.6 201.9 %all-reduce.7.cloned.1.call-start = ((), (), s32[]{:S(2)}) async-start(), calls=%async_computation.3 | async-start | bytes 524288 | tf_op jit(solution)/shard_map/psum | solution.py:139
  216.6 9.5 collective-permute-start.2
  222.5 7.9 collective-permute-start.3
  367.4 198.6 %all-gather.9.cloned.1.call-start = ((), (), s32[]{:S(2)}) async-start(), calls=%async_computation.4 | async-start | bytes 2113536 | tf_op jit(solution)/shard_map/all_gather | solution.py:134
  420.5 201.8 %all-reduce.9.cloned.1.call-start = ((), (), s32[]{:S(2)}) async-start(), calls=%async_computation.5 | async-start | bytes 524288 | tf_op jit(solution)/shard_map/psum | solution.py:139
  420.5 9.5 collective-permute-start.4
  426.4 7.9 collective-permute-start.5
  571.1 198.8 %all-gather.11.cloned.1.call-start = ((), (), s32[]{:S(2)}) async-start(), calls=%async_computation.6 | async-start | bytes 2113536 | tf_op jit(solution)/shard_map/all_gather | solution.py:134
  624.2 201.9 %all-reduce.11.cloned.1.call-start = ((), (), s32[]{:S(2)}) async-start(), calls=%async_computation.7 | async-start | bytes 524288 | tf_op jit(solution)/shard_map/psum | solution.py:139
  624.3 9.5 collective-permute-start.6
  630.2 7.9 collective-permute-start.7
  639.9 135.1 %copy-start.2 = (f32[512,128]{1,0:T(8,128)S(1)}, f32[512,128]{1,0:T(8,128)}, u32[]{:S(2)}) copy-start(f32[512,128]{1,0:T(8,128)} %param.13) | copy-start | bytes 786436
  772.8 3.9 copy-start.10
  773.2 4.3 copy-start.3
  773.3 5.3 copy-start.4
  774.1 5.5 copy-start.5
  834.4 499.5 %copy-start.6 = (f32[512,128]{0,1:T(8,128)S(1)}, f32[512,128]{0,1:T(8,128)}, u32[]{:S(2)}) copy-start(f32[512,128]{0,1:T(8,128)} %copy.65) | copy-start | bytes 786436
  834.4 499.5 %copy-start.7 = (f32[512,128]{0,1:T(8,128)S(1)}, f32[512,128]{0,1:T(8,128)}, u32[]{:S(2)}) copy-start(f32[512,128]{0,1:T(8,128)} %copy.66) | copy-start | bytes 786436
  1335.0 0.6 copy-start.11
Sparse Core Ops, SparseCore 0:
  11.7 146.4 all-gather.4
  163.5 50.9 all-reduce.4
  218.3 143.8 all-gather.6
  367.5 50.9 all-reduce.6
  422.0 143.8 all-gather.8
  571.2 50.9 all-reduce.8
  626.0 143.8 all-gather.10
  775.2 50.9 all-reduce.10
where the time goes:
time: 1350 us; the launch traced here: 1340 us
  waiting for transfers between devices  742 us (55%)
  blocking collectives  492 us (36%)
  starting transfers between devices  33.9 us (3%)
  local copies, waits for them, and re-layouts  30.2 us (2%)
  matrix products  16.2 us (1%)
  between operations  14.7 us (1%)
  other arithmetic  13.6 us (1%)
    all_gather x4, waiting for transfers between devices, local(): table = lax.all_gather(coeffs, 'row', axis=0, tiled=True)  524 us
    psum x1, blocking collectives, local(): gram_sum = lax.psum(local_gram, 'row')  492 us
    psum x4, waiting for transfers between devices, local(): current = lax.psum(partial_value, 'col')  199 us
  transfers between devices with their start and end apart: 16, of which 15 were waited for; matrix products, arithmetic and copies ran while one was open for 1% of the time, Pallas kernels for 0%

commit v1 on v0

v1 whole, which is shorter than its diff:
```python
import functools

import jax
import jax.numpy as jnp
from jax import lax
from jax.experimental import pallas as pl
from jax.experimental.pallas import tpu as pltpu
from jax.sharding import PartitionSpec as P

LEAF_UNKNOWNS = 256
CL_DEV = 2
REACH = 2
SB = 4
RANK = 16
LANES = 128
NY, NZ, NC = 4, 16, 2
NX = 4
NROW = NY * NZ * NC
WIDTH = LANES // NX
ROWS = CL_DEV * LEAF_UNKNOWNS
SLOTS = 16
FAR = SLOTS * NX
PAIRS = [(a, b) for a in range(SB + 1) for b in range(a, SB + 1)]


HIGH = lax.Precision.HIGHEST
SHIFT = 1.0
MESH = pl.DeviceIdType.MESH


def cholesky_upper(entries, order_n):
    zero_entry = jnp.zeros_like(entries[0][0])
    upper_r = []
    for row_idx in range(order_n):
        upper_r.append([zero_entry] * order_n)
    for row_idx in range(order_n):
        running = entries[row_idx][row_idx]
        for earlier in range(row_idx):
            running = running - upper_r[earlier][row_idx] * upper_r[earlier][row_idx]
        pivot_val = jnp.sqrt(running)
        upper_r[row_idx][row_idx] = pivot_val
        for col_idx in range(row_idx + 1, order_n):
            entry_val = entries[row_idx][col_idx]
            for earlier in range(row_idx):
                entry_val = entry_val - upper_r[earlier][row_idx] * upper_r[earlier][col_idx]
            upper_r[row_idx][col_idx] = entry_val / pivot_val
    return upper_r


def small_update(gram_sum, scale_factor, depth_n):
    order_n = depth_n + 1
    entries = gram_sum
    upper_r = cholesky_upper(entries, order_n)
    shifted = [
        [
            SHIFT * upper_r[row_idx][col_idx] + upper_r[row_idx][col_idx + 1]
            for col_idx in range(depth_n)
        ]
        for row_idx in range(order_n)
    ]
    hessen = []
    for row_idx in range(order_n):
        row_vals = []
        for col_idx in range(depth_n):
            entry_val = shifted[row_idx][col_idx]
            for earlier in range(col_idx):
                entry_val = entry_val - row_vals[earlier] * upper_r[earlier][col_idx]
            row_vals.append(entry_val / upper_r[col_idx][col_idx])
        hessen.append(row_vals)
    normal = []
    for row_idx in range(depth_n):
        row_vals = []
        for col_idx in range(depth_n):
            entry_val = hessen[0][row_idx] * hessen[0][col_idx]
            for inner in range(1, order_n):
                entry_val = entry_val + hessen[inner][row_idx] * hessen[inner][col_idx]
            row_vals.append(entry_val)
        normal.append(row_vals)
    target = [scale_factor * upper_r[0][0] * hessen[0][col_idx] for col_idx in range(depth_n)]
    factor = cholesky_upper(normal, depth_n)
    forward = []
    for row_idx in range(depth_n):
        entry_val = target[row_idx]
        for earlier in range(row_idx):
            entry_val = entry_val - factor[earlier][row_idx] * forward[earlier]
        forward.append(entry_val / factor[row_idx][row_idx])
    solved = [None] * depth_n
    for row_idx in range(depth_n - 1, -1, -1):
        entry_val = forward[row_idx]
        for later in range(row_idx + 1, depth_n):
            entry_val = entry_val - factor[row_idx][later] * solved[later]
        solved[row_idx] = entry_val / factor[row_idx][row_idx]
    weights = [None] * depth_n
    for row_idx in range(depth_n - 1, -1, -1):
        entry_val = solved[row_idx]
        for later in range(row_idx + 1, depth_n):
            entry_val = entry_val - upper_r[row_idx][later] * weights[later]
        weights[row_idx] = entry_val / upper_r[row_idx][row_idx]
    return (hessen, weights)


def dot(left, right):
    return jnp.dot(left, right, precision=HIGH, preferred_element_type=jnp.float32)


def lane_group(shape):
    return lax.broadcasted_iota(jnp.int32, shape, 1) // WIDTH


def pack(pieces):
    group = lane_group(pieces[0].shape)
    out = pieces[0]
    for q in range(1, len(pieces)):
        out = jnp.where(group == q, pltpu.roll(pieces[q], q * WIDTH, 1), out)
    return out


def lanes_to_front(value, q):
    return value if q == 0 else pltpu.roll(value, LANES - q * WIDTH, 1)


def kernel(
    idx, res, sol, near, coup, cb, rbt, out, hout,
    W, T, U, HP, HB, H, F, NB, CP, GR, GZ, GY, GC, XO, XH,
    z_send, z_recv, y_send, y_recv, c_send, c_recv, h_send, h_recv,
    n_send, n_recv, p_send, p_recv, o_send, o_recv, q_send, q_recv,
):
    row = lax.axis_index("row")
    col = lax.axis_index("col")
    core = row % NC
    zz = (row // NC) % NZ
    yy = row // (NC * NZ)
    z_dev = [(yy * NZ + (zz + d) % NZ) * NC + core for d in range(NZ)]
    y_dev = [(((yy + d) % NY) * NZ + zz) * NC + core for d in range(NY)]
    mate = row + 1 - 2 * core
    above = (row + 1) % NROW
    below = (row + NROW - 1) % NROW
    x_dev = [(col + d) % NX for d in range(NX)]

    barrier = pltpu.get_barrier_semaphore()
    for dev in z_dev[1:] + y_dev[1:] + [mate, above, below]:
        pl.semaphore_signal(barrier, inc=1, device_id={"row": dev}, device_id_type=MESH)
    for dev in x_dev[1:]:
        pl.semaphore_signal(barrier, inc=1, device_id={"col": dev}, device_id_type=MESH)

    def to_row(src, dst, send, recv, dev):
        return pltpu.make_async_remote_copy(
            src_ref=src, dst_ref=dst, send_sem=send, recv_sem=recv,
            device_id={"row": dev}, device_id_type=MESH,
        )

    def to_col(src, dst, send, recv, dev):
        return pltpu.make_async_remote_copy(
            src_ref=src, dst_ref=dst, send_sem=send, recv_sem=recv,
            device_id={"col": dev}, device_id_type=MESH,
        )

    W[0] = pltpu.roll(res[...], (LANES - col * WIDTH) % LANES, 1)

    def stage_table(k):
        pieces = []
        for c in range(CL_DEV):
            value = dot(cb[c], W[k, pl.ds(c * LEAF_UNKNOWNS, LEAF_UNKNOWNS), :])
            pieces += [value[0:8], value[8:16]]
        T[k, 0, 0, 0] = pack(pieces)

    def stage_halo(k):
        HP[k] = pack([W[k, pl.ds(q * LANES, LANES), :] for q in range(4)])

    stage_table(0)
    stage_halo(0)
    pl.semaphore_wait(barrier, (NZ - 1) + (NY - 1) + 3 + (NX - 1))

    near_out = [
        to_col(near, NB.at[d - 1], n_send.at[d - 1], n_recv.at[d - 1], x_dev[d])
        for d in range(1, NX)
    ]
    coup_out = [
        to_col(coup, CP.at[d - 1], p_send.at[d - 1], p_recv.at[d - 1], x_dev[d])
        for d in range(1, NX)
    ]

    def unpack_table(k, side):
        def one(n, carry):
            value = T[k, side, n // NZ, n % NZ]
            for q in range(4):
                where = side * CL_DEV * NY * NZ + n * CL_DEV + q // 2
                U[where, pl.ds((q % 2) * 8, 8), :] = lanes_to_front(value, q)
            return carry

        lax.fori_loop(0, NY * NZ, one, 0, unroll=8)

    def near_product(k):
        for q in range(4):
            rows = pl.ds((q % 2) * LANES, LANES)
            H[q // 2, rows, :] = lanes_to_front(HB[k, 0], q)
            H[4 + q // 2, rows, :] = lanes_to_front(HB[k, 1], q)
        for c in range(CL_DEV):
            H[2 + c] = W[k, pl.ds(c * LEAF_UNKNOWNS, LEAF_UNKNOWNS), :]
        for c in range(CL_DEV):
            base = CL_DEV * FAR + c * NX
            total = dot(near[c], H[idx[base]])
            for s in range(1, NX):
                total = total + dot(NB[s - 1, c], H[idx[base + s]])
            W[k + 1, pl.ds(c * LEAF_UNKNOWNS, LEAF_UNKNOWNS), :] = total

    def step(k, carry):
        z_out = [
            to_row(T.at[k, 0, 0, 0], T.at[k, 0, 0, d], z_send.at[k], z_recv.at[k], z_dev[d])
            for d in range(1, NZ)
        ]
        z_all = to_row(
            T.at[k, 0, 0, pl.ds(1, NZ - 1)], T.at[k, 0, 0, pl.ds(1, NZ - 1)],
            z_send.at[k], z_recv.at[k], z_dev[1],
        )
        y_out = [
            to_row(T.at[k, 0, 0], T.at[k, 0, d], y_send.at[k, d - 1], y_recv.at[k, d - 1], y_dev[d])
            for d in range(1, NY)
        ]
        c_out = to_row(T.at[k, 0], T.at[k, 1], c_send.at[k], c_recv.at[k], mate)
        halo_out = [
            to_row(HP.at[k], HB.at[k, 0], h_send.at[k, 0], h_recv.at[k, 0], above),
            to_row(HP.at[k], HB.at[k, 1], h_send.at[k, 1], h_recv.at[k, 1], below),
        ]
        for copy in z_out:
            copy.start()
        for copy in halo_out:
            copy.start()

        @pl.when(k == 0)
        def _():
            for copy in coup_out:
                copy.start()
            for copy in near_out:
                copy.start()

        for copy in halo_out:
            copy.wait()

        @pl.when(k > 0)
        def _():
            near_product(k)

        z_all.wait_recv()
        for copy in y_out:
            copy.start()
        for copy in y_out:
            copy.wait_recv()
        c_out.start()
        unpack_table(k, 0)

        @pl.when(k == 0)
        def _():
            for copy in coup_out:
                copy.wait()
            for copy in near_out:
                copy.wait()
            near_product(k)

        c_out.wait()
        for copy in y_out:
            copy.wait_send()
        z_all.wait_send()
        unpack_table(k, 1)

        for c in range(CL_DEV):

            def fetch(p, carry, c=c):
                F[c, pl.ds(p * RANK, RANK), :] = U[idx[c * FAR + p]]
                return carry

            lax.fori_loop(0, FAR, fetch, 0, unroll=8)
        span = SLOTS * RANK
        for c in range(CL_DEV):
            rows = pl.ds(c * RANK, RANK)
            total = dot(coup[rows, :], F[c, pl.ds(0, span), :])
            for s in range(1, NX):
                total = total + dot(CP[s - 1, rows, :], F[c, pl.ds(s * span, span), :])
            W[k + 1, pl.ds(c * LEAF_UNKNOWNS, LEAF_UNKNOWNS), :] += dot(rbt[c], total)

        @pl.when(k < SB - 1)
        def _():
            stage_table(k + 1)
            stage_halo(k + 1)

        return carry

    lax.fori_loop(0, SB, step, 0)

    chunk = 32

    def gather_gram(n, sums):
        vals = [W[a, pl.ds(n * chunk, chunk), :] for a in range(SB + 1)]
        new = []
        for (a, b), old in zip(PAIRS, sums):
            prod = vals[a] * vals[b]
            new.append(old + ((prod[0:8] + prod[8:16]) + (prod[16:24] + prod[24:32])))
        return tuple(new)

    sums = lax.fori_loop(
        0, ROWS // chunk, gather_gram, tuple(jnp.zeros((8, LANES), jnp.float32) for _ in PAIRS)
    )
    GR[...] = jnp.zeros_like(GR)
    for n, value in enumerate(sums):
        GR[pl.ds(n, 1), :] = jnp.sum(value, axis=0, keepdims=True)
    grams = GR[...]
    GZ[0] = pack([grams[0:8], grams[8:16]])
    z_out = [
        to_row(GZ.at[0], GZ.at[d], z_send.at[SB], z_recv.at[SB], z_dev[d]) for d in range(1, NZ)
    ]
    z_all = to_row(
        GZ.at[pl.ds(1, NZ - 1)], GZ.at[pl.ds(1, NZ - 1)], z_send.at[SB], z_recv.at[SB], z_dev[1]
    )
    for copy in z_out:
        copy.start()
    z_all.wait()
    total = GZ[zz % NZ]
    for src in range(1, NZ):
        total = total + GZ[(zz + NZ - src) % NZ]
    GY[0] = total
    y_out = [
        to_row(GY.at[0], GY.at[d], y_send.at[SB, d - 1], y_recv.at[SB, d - 1], y_dev[d])
        for d in range(1, NY)
    ]
    for copy in y_out:
        copy.start()
    for copy in y_out:
        copy.wait()
    total = GY[yy % NY]
    for src in range(1, NY):
        total = total + GY[(yy + NY - src) % NY]
    GC[0] = total
    c_out = to_row(GC.at[0], GC.at[1], c_send.at[SB], c_recv.at[SB], mate)
    c_out.start()
    c_out.wait()
    total = GC[0] + GC[1]
    second = lanes_to_front(total, 1)
    gram = [[None] * (SB + 1) for _ in range(SB + 1)]
    for n, (a, b) in enumerate(PAIRS):
        gram[a][b] = gram[b][a] = total[n : n + 1] if n < 8 else second[n - 8 : n - 7]
    hessen, weights = small_update(gram, 1.0, SB)
    XH[0] = jnp.zeros((24, LANES), jnp.float32)
    for a in range(SB + 1):
        for b in range(SB):
            XH[0, pl.ds(a * SB + b, 1), :] = hessen[a][b]
    pieces = []
    for q in range(4):
        rows = pl.ds(q * LANES, LANES)
        value = weights[0] * W[0, rows, :]
        for k in range(1, SB):
            value = value + weights[k] * W[k, rows, :]
        pieces.append(value)
    XO[0] = pack(pieces)
    last = []
    for d in range(1, NX):
        last.append(to_col(XO.at[0], XO.at[d], o_send.at[d - 1], o_recv.at[d - 1], x_dev[d]))
        last.append(to_col(XH.at[0], XH.at[d], q_send.at[d - 1], q_recv.at[d - 1], x_dev[d]))
    for copy in last:
        copy.start()
    for copy in last:
        copy.wait()
    group = lane_group((LANES, LANES))
    values = [XO[(col + NX - src) % NX] for src in range(NX)]
    for q in range(4):
        rows = pl.ds(q * LANES, LANES)
        value = lanes_to_front(values[0], q)
        for src in range(1, NX):
            shift = ((src - q) * WIDTH) % LANES
            moved = pltpu.roll(values[src], shift, 1) if shift else values[src]
            value = jnp.where(group == src, moved, value)
        out[rows, :] = sol[rows, :] + value
    hout[...] = pack([XH[(col + NX - src) % NX] for src in range(NX)])


def local(
    residual,
    solution,
    near_field_blocks,
    near_cols,
    couplings,
    far_cols,
    far_count,
    col_basis,
    row_basis,
):
    row = lax.axis_index("row")
    col = lax.axis_index("col")
    positions = col * SLOTS + jnp.arange(SLOTS, dtype=jnp.int32)
    live = positions[None, :] < far_count[:, None]
    weighted = jnp.where(live[:, :, None, None], couplings, 0.0)
    weighted = weighted.transpose(0, 2, 1, 3).reshape(CL_DEV * RANK, SLOTS * RANK)
    own = jnp.concatenate([far_cols, near_cols], axis=1)
    lists = [own] + [
        lax.ppermute(own, "col", [(i, (i + s) % NX) for i in range(NX)]) for s in range(1, NX)
    ]
    far = jnp.concatenate([piece[:, :SLOTS] for piece in lists], axis=1)
    near = jnp.concatenate([piece[:, SLOTS:] for piece in lists], axis=1)
    owner = far // CL_DEV
    core, rest = owner % NC, owner // NC
    tile = (
        ((row + NC - core) % NC) * (NY * NZ)
        + ((row // (NC * NZ) + NY - rest // NZ) % NY) * NZ
        + (row // NC + NZ - rest % NZ) % NZ
    )
    idx = jnp.concatenate(
        [
            (tile * CL_DEV + far % CL_DEV).reshape(-1),
            (near - (row * CL_DEV - REACH)).reshape(-1),
        ]
    ).astype(jnp.int32)
    f32 = jnp.float32
    vmem = pl.BlockSpec(memory_space=pltpu.VMEM)
    dma = pltpu.SemaphoreType.DMA
    new_sol, hess = pl.pallas_call(
        kernel,
        out_shape=(
            jax.ShapeDtypeStruct((ROWS, LANES), f32),
            jax.ShapeDtypeStruct((24, LANES), f32),
        ),
        in_specs=[pl.BlockSpec(memory_space=pltpu.SMEM)] + [vmem] * 6,
        out_specs=(vmem, vmem),
        scratch_shapes=[
            pltpu.VMEM((SB + 1, ROWS, LANES), f32),
            pltpu.VMEM((SB, NC, NY, NZ, 8, LANES), f32),
            pltpu.VMEM((NROW * CL_DEV, RANK, LANES), f32),
            pltpu.VMEM((SB, LANES, LANES), f32),
            pltpu.VMEM((SB, 2, LANES, LANES), f32),
            pltpu.VMEM((CL_DEV + 2 * REACH, LEAF_UNKNOWNS, LANES), f32),
            pltpu.VMEM((CL_DEV, FAR * RANK, LANES), f32),
            pltpu.VMEM((NX - 1, CL_DEV, LEAF_UNKNOWNS, LEAF_UNKNOWNS), f32),
            pltpu.VMEM((NX - 1, CL_DEV * RANK, SLOTS * RANK), f32),
            pltpu.VMEM((16, LANES), f32),
            pltpu.VMEM((NZ, 8, LANES), f32),
            pltpu.VMEM((NY, 8, LANES), f32),
            pltpu.VMEM((NC, 8, LANES), f32),
            pltpu.VMEM((NX, LANES, LANES), f32),
            pltpu.VMEM((NX, 24, LANES), f32),
            dma((SB + 1,)), dma((SB + 1,)),
            dma((SB + 1, NY - 1)), dma((SB + 1, NY - 1)),
            dma((SB + 1,)), dma((SB + 1,)),
            dma((SB, 2)), dma((SB, 2)),
            dma((NX - 1,)), dma((NX - 1,)),
            dma((NX - 1,)), dma((NX - 1,)),
            dma((NX - 1,)), dma((NX - 1,)),
            dma((NX - 1,)), dma((NX - 1,)),
        ],
        compiler_params=pltpu.CompilerParams(
            collective_id=0, has_side_effects=True, vmem_limit_bytes=48 * 1024 * 1024
        ),
    )(
        idx,
        residual,
        solution,
        near_field_blocks.reshape(CL_DEV, LEAF_UNKNOWNS, LEAF_UNKNOWNS),
        weighted,
        col_basis,
        row_basis.transpose(0, 2, 1),
    )
    return (new_sol, hess[: (SB + 1) * SB].reshape(SB + 1, SB, LANES))


def solution(mesh):
    placed = (
        P("row", None),
        P("row", None),
        P("row", "col", None, None),
        P("row", "col"),
        P("row", "col", None, None),
        P("row", "col"),
        P("row"),
        P("row", None, None),
        P("row", None, None),
    )
    return jax.shard_map(
        local, mesh=mesh, in_specs=placed, out_specs=(P("row", None), P()), check_vma=False
    )
```

time: 1350 us -> 137 us (0.10)
  waiting for transfers between devices: 742 us -> 0.27 us
  blocking collectives: 492 us -> 0 us
  Pallas kernels: 0 us -> 120 us
  local copies, waits for them, and re-layouts: 30.2 us -> 3.94 us
  starting transfers between devices: 33.9 us -> 10.1 us
  matrix products: 16.2 us -> 0 us
  between operations: 14.7 us -> 0.84 us
    all_gather x4 -> x0, waiting for transfers between devices: 524 us -> none  [local(): table = lax.all_gather(coeffs, 'row', axis=0, tiled=True)]
    psum x1 -> x0, blocking collectives: 492 us -> none  [local(): gram_sum = lax.psum(local_gram, 'row')]
    psum x4 -> x0, waiting for transfers between devices: 199 us -> none  [local(): current = lax.psum(partial_value, 'col')]
    pallas_call x0 -> x1, Pallas kernels: none -> 120 us  [local(): pl.pallas_call(kernel, out_shape=(jax.ShapeDtypeStruct((ROWS, LANES), f32...]
    ppermute x8 -> x3, starting transfers between devices: 33.6 us -> 10.1 us  [local(): lax.ppermute(own, 'col', [(i, (i + s) % NX) for i in range(NX)])]
    ppermute x8 -> x3, waiting for transfers between devices: 18.3 us -> 0.27 us  [local(): lax.ppermute(own, 'col', [(i, (i + s) % NX) for i in range(NX)])]
    dot_general x17 -> x0, matrix products: 16.2 us -> none  [the longest x4 4.5 us: local(): coeffs = jnp.einsum('ckb,cbr->ckr', col_basis, own_panels, precision=HIGH)]
  transfers between devices with their start and end apart: 16 -> 3, of which waited for: 15 -> 1; matrix products, arithmetic and copies ran while one was open for 1% -> 1% of each run, Pallas kernels for 0% -> 0%
where the time goes in v1:
time: 137 us
  Pallas kernels  120 us (88%)
  starting transfers between devices  10.1 us (7%)
  local copies, waits for them, and re-layouts  3.94 us (3%)
  other arithmetic  1.4 us (1%)
    pallas_call x1, Pallas kernels, local(): pl.pallas_call(kernel, out_shape=(jax.ShapeDtypeStruct((ROWS, LANES), f32...  120 us
    ppermute x3, starting transfers between devices, local(): lax.ppermute(own, 'col', [(i, (i + s) % NX) for i in range(NX)])  10.1 us
  transfers between devices with their start and end apart: 3, of which 1 were waited for; matrix products, arithmetic and copies ran while one was open for 1% of the time, Pallas kernels for 0%

profile of v1, /device:TPU:1, one launch (start us, length us, event | category | flops | bytes accessed | tf_op | source)
XLA Modules:
  0.0 137.0 jit_solution(17688291329121113003)
XLA Ops:
  0.6 0.0 copy-start.5
  0.6 0.7 copy.11
  1.4 0.0 copy-done.5
  1.4 0.1 pad_add_fusion
  1.5 5.2 %collective-permute-start.2 = (s32[2,17]{1,0:T(2,128)S(1)}, s32[2,17]{1,0:T(2,128)S(1)}, u32[]{:S(2)}, u32[]{:S(2)}) collective-permute-start(s32[2,17]{1,0:T(2,128)S(1)} %pad_add_fusion), channel_id=1, source_target_pairs={{0,3},{1,0},{2,1},{3,2},{4,7},{5,4},{6,5},{7,6},{8,11},{9,8},{10,9... | collective-permute-start | bytes 416 | tf_op jit(solution)/shard_map/ppermute | solution.py:394
  6.7 2.4 %collective-permute-start.1 = (s32[2,17]{1,0:T(2,128)S(1)}, s32[2,17]{1,0:T(2,128)S(1)}, u32[]{:S(2)}, u32[]{:S(2)}) collective-permute-start(s32[2,17]{1,0:T(2,128)S(1)} %pad_add_fusion), channel_id=1, source_target_pairs={{0,2},{1,3},{2,0},{3,1},{4,6},{5,7},{6,4},{7,5},{8,10},{9,11},{10,... | collective-permute-start | bytes 416 | tf_op jit(solution)/shard_map/ppermute | solution.py:394
  9.1 2.5 %collective-permute-start = (s32[2,17]{1,0:T(2,128)S(1)}, s32[2,17]{1,0:T(2,128)S(1)}, u32[]{:S(2)}, u32[]{:S(2)}) collective-permute-start(s32[2,17]{1,0:T(2,128)S(1)} %pad_add_fusion), channel_id=1, source_target_pairs={{0,1},{1,2},{2,3},{3,0},{4,5},{5,6},{6,7},{7,4},{8,9},{9,10},{10,1... | collective-permute-start | bytes 416 | tf_op jit(solution)/shard_map/ppermute | solution.py:394
  11.6 0.0 copy-start.6
  11.7 0.6 copy-done.6
  12.3 0.1 broadcast_compare_fusion
  12.4 1.0 select_bitcast_fusion
  13.4 0.0 copy-start.4
  13.4 0.0 copy-start
  13.5 0.1 copy.13
  13.5 0.0 copy-start.1
  13.6 0.0 copy-start.2
  13.6 0.1 reshape.52.coup
  13.7 0.5 copy-done.4
  14.2 0.1 copy.14
  14.3 0.0 copy-start.3
  14.3 0.0 collective-permute-done.2
  14.4 0.0 collective-permute-done.1
  14.4 0.3 collective-permute-done
  14.6 0.1 pad_add_fusion.1
  14.7 0.1 concatenate.16
  14.8 0.1 slice.26
  14.9 0.1 slice.25
  14.9 0.1 slice.24
  15.0 0.1 add_subtract_fusion
  15.1 0.1 sub.69
  15.2 0.0 copy-done
  15.2 0.0 copy-done.1
  15.2 0.0 copy-done.2
  15.3 0.0 copy-done.3
  15.3 120.4 %shard_map.104 = (f32[512,128]{1,0:T(8,128)S(1)}, f32[24,128]{1,0:T(8,128)S(1)}) custom-call(s32[136]{0:T(256)S(1)} %pad_add_fusion.2.idx, f32[512,128]{1,0:T(8,128)S(1)} %copy-done.1, f32[512,128]{1,0:T(8,128)S(1)} %copy-done.2, f32[2,256,256]{2,1,0:T(8,128)S(1)} %bitcast.11, f32[32,256]{1,0:T(8,128)S(1)} %reshape.52.coup, f32[2,16,256]{2,1,0:T(8,128)S(1)} %copy-done.3, ...), custom_call_target="tpu_custom_call" | custom-call | tf_op jit(solution)/shard_map/pallas_call | solution.py:414
  135.7 0.6 reshape.53
  136.3 0.7 copy.16
  (3 shorter events, 0.1 us)
Async XLA Ops:
  0.6 0.8 copy-start.5
  1.5 12.9 %collective-permute-start.2 = (s32[2,17]{1,0:T(2,128)S(1)}, s32[2,17]{1,0:T(2,128)S(1)}, u32[]{:S(2)}, u32[]{:S(2)}) collective-permute-start(s32[2,17]{1,0:T(2,128)S(1)} %pad_add_fusion), channel_id=1, source_target_pairs={{0,3},{1,0},{2,1},{3,2},{4,7},{5,4},{6,5},{7,6},{8,11},{9,8},{10,9... | collective-permute-start | bytes 416 | tf_op jit(solution)/shard_map/ppermute | solution.py:394
  6.7 7.7 %collective-permute-start.1 = (s32[2,17]{1,0:T(2,128)S(1)}, s32[2,17]{1,0:T(2,128)S(1)}, u32[]{:S(2)}, u32[]{:S(2)}) collective-permute-start(s32[2,17]{1,0:T(2,128)S(1)} %pad_add_fusion), channel_id=1, source_target_pairs={{0,2},{1,3},{2,0},{3,1},{4,6},{5,7},{6,4},{7,5},{8,10},{9,11},{10,... | collective-permute-start | bytes 416 | tf_op jit(solution)/shard_map/ppermute | solution.py:394
  9.1 5.5 %collective-permute-start = (s32[2,17]{1,0:T(2,128)S(1)}, s32[2,17]{1,0:T(2,128)S(1)}, u32[]{:S(2)}, u32[]{:S(2)}) collective-permute-start(s32[2,17]{1,0:T(2,128)S(1)} %pad_add_fusion), channel_id=1, source_target_pairs={{0,1},{1,2},{2,3},{3,0},{4,5},{5,6},{6,7},{7,4},{8,9},{9,10},{10,1... | collective-permute-start | bytes 416 | tf_op jit(solution)/shard_map/ppermute | solution.py:394
  11.6 0.7 copy-start.6
  13.4 0.8 copy-start.4
  13.4 1.8 %copy-start = (f32[2,1,256,256]{3,2,1,0:T(8,128)S(1)}, f32[2,1,256,256]{3,2,1,0:T(8,128)}, u32[]{:S(2)}) copy-start(f32[2,1,256,256]{3,2,1,0:T(8,128)} %param.11) | copy-start | bytes 1572868
  13.5 1.7 %copy-start.1 = (f32[512,128]{1,0:T(8,128)S(1)}, f32[512,128]{1,0:T(8,128)}, u32[]{:S(2)}) copy-start(f32[512,128]{1,0:T(8,128)} %res.1) | copy-start | bytes 786436
  13.6 1.7 %copy-start.2 = (f32[512,128]{1,0:T(8,128)S(1)}, f32[512,128]{1,0:T(8,128)}, u32[]{:S(2)}) copy-start(f32[512,128]{1,0:T(8,128)} %sol.1) | copy-start | bytes 786436
  14.3 0.9 copy-start.3

commit v2 on v1

--- a/solution.py
+++ b/solution.py
@@ -20,6 +20,12 @@
 ROWS = CL_DEV * LEAF_UNKNOWNS
 SLOTS = 16
 FAR = SLOTS * NX
+REACH_Z = NZ // 4
+RUNS = [
+    run
+    for run in ((0, REACH_Z + 1), (NZ - REACH_Z, NZ), (REACH_Z + 1, NZ - REACH_Z))
+    if run[1] > run[0]
+]
 PAIRS = [(a, b) for a in range(SB + 1) for b in range(a, SB + 1)]
 
 
@@ -120,10 +126,11 @@
 
 
 def kernel(
-    idx, res, sol, near, coup, cb, rbt, out, hout,
-    W, T, U, HP, HB, H, F, NB, CP, GR, GZ, GY, GC, XO, XH,
+    lists, res, sol, near, coup, cb, rbt, out, hout,
+    W, T, U, HP, HB, H, F, NB, CP, GR, GZ, GY, GC, XO, XH, IV, IX,
     z_send, z_recv, y_send, y_recv, c_send, c_recv, h_send, h_recv,
     n_send, n_recv, p_send, p_recv, o_send, o_recv, q_send, q_recv,
+    i_send, i_recv, i_copy,
 ):
     row = lax.axis_index("row")
     col = lax.axis_index("col")
@@ -171,24 +178,46 @@
     stage_halo(0)
     pl.semaphore_wait(barrier, (NZ - 1) + (NY - 1) + 3 + (NX - 1))
 
-    near_out = [
-        to_col(near, NB.at[d - 1], n_send.at[d - 1], n_recv.at[d - 1], x_dev[d])
+    right, left = x_dev[1], x_dev[NX - 1]
+
+    def near_copy(n, src, dst, dev):
+        return to_col(src, dst, n_send.at[n], n_recv.at[n], dev)
+
+    near_first = [
+        near_copy(0, near.at[0], NB.at[0, 0], right),
+        near_copy(1, near.at[1], NB.at[2, 1], left),
+    ]
+    near_second = [
+        near_copy(2, near.at[1], NB.at[0, 1], right),
+        near_copy(3, near.at[0], NB.at[2, 0], left),
+    ]
+    near_relay = [
+        near_copy(4, NB.at[0, 0], NB.at[1, 0], right),
+        near_copy(5, NB.at[2, 1], NB.at[1, 1], left),
+    ]
+    list_out = [
+        to_col(lists, IV.at[d - 1], i_send.at[d - 1], i_recv.at[d - 1], x_dev[d])
         for d in range(1, NX)
+    ]
+    list_in = [
+        pltpu.make_async_copy(lists if d == 0 else IV.at[d - 1], IX.at[d], i_copy.at[d])
+        for d in range(NX)
     ]
     coup_out = [
         to_col(coup, CP.at[d - 1], p_send.at[d - 1], p_recv.at[d - 1], x_dev[d])
         for d in range(1, NX)
     ]
 
-    def unpack_table(k, side):
+    def unpack_table(k, side, run):
         def one(n, carry):
-            value = T[k, side, n // NZ, n % NZ]
-            for q in range(4):
-                where = side * CL_DEV * NY * NZ + n * CL_DEV + q // 2
-                U[where, pl.ds((q % 2) * 8, 8), :] = lanes_to_front(value, q)
+            for y in range(NY):
+                value = T[k, side, y, n]
+                for q in range(4):
+                    where = ((side * NY + y) * NZ + n) * CL_DEV + q // 2
+                    U[where, pl.ds((q % 2) * 8, 8), :] = lanes_to_front(value, q)
             return carry
 
-        lax.fori_loop(0, NY * NZ, one, 0, unroll=8)
+        lax.fori_loop(run[0], run[1], one, 0)
 
     def near_product(k):
         for q in range(4):
@@ -198,26 +227,43 @@
         for c in range(CL_DEV):
             H[2 + c] = W[k, pl.ds(c * LEAF_UNKNOWNS, LEAF_UNKNOWNS), :]
         for c in range(CL_DEV):
-            base = CL_DEV * FAR + c * NX
-            total = dot(near[c], H[idx[base]])
+            total = dot(near[c], H[IX[0, c, SLOTS]])
             for s in range(1, NX):
-                total = total + dot(NB[s - 1, c], H[idx[base + s]])
+                total = total + dot(NB[s - 1, c], H[IX[s, c, SLOTS]])
             W[k + 1, pl.ds(c * LEAF_UNKNOWNS, LEAF_UNKNOWNS), :] = total
 
     def step(k, carry):
         z_out = [
-            to_row(T.at[k, 0, 0, 0], T.at[k, 0, 0, d], z_send.at[k], z_recv.at[k], z_dev[d])
-            for d in range(1, NZ)
+            to_row(
+                T.at[k, 0, 0, 0], T.at[k, 0, 0, d], z_send.at[k],
+                z_recv.at[k, [d >= lo and d < hi for lo, hi in RUNS].index(True)], z_dev[d],
+            )
+            for d in sorted(range(1, NZ), key=lambda d: -min(d, NZ - d))
         ]
         z_all = to_row(
             T.at[k, 0, 0, pl.ds(1, NZ - 1)], T.at[k, 0, 0, pl.ds(1, NZ - 1)],
-            z_send.at[k], z_recv.at[k], z_dev[1],
+            z_send.at[k], z_recv.at[k, 0], z_dev[1],
         )
-        y_out = [
-            to_row(T.at[k, 0, 0], T.at[k, 0, d], y_send.at[k, d - 1], y_recv.at[k, d - 1], y_dev[d])
-            for d in range(1, NY)
-        ]
-        c_out = to_row(T.at[k, 0], T.at[k, 1], c_send.at[k], c_recv.at[k], mate)
+        z_in, y_out, c_out = [], [], []
+        for n, (lo, hi) in enumerate(RUNS):
+            got = pl.ds(max(lo, 1), hi - max(lo, 1))
+            z_in.append(
+                to_row(T.at[k, 0, 0, got], T.at[k, 0, 0, got], z_send.at[k], z_recv.at[k, n], z_dev[1])
+                if hi > 1 else None
+            )
+            run = pl.ds(lo, hi - lo)
+            y_out.append([
+                to_row(
+                    T.at[k, 0, 0, run], T.at[k, 0, d, run],
+                    y_send.at[k, n, d - 1], y_recv.at[k, n, d - 1], y_dev[d],
+                )
+                for d in range(1, NY)
+            ])
+            c_out.append(
+                to_row(
+                    T.at[k, 0, :, run], T.at[k, 1, :, run], c_send.at[k, n], c_recv.at[k, n], mate
+                )
+            )
         halo_out = [
             to_row(HP.at[k], HB.at[k, 0], h_send.at[k, 0], h_recv.at[k, 0], above),
             to_row(HP.at[k], HB.at[k, 1], h_send.at[k, 1], h_recv.at[k, 1], below),
@@ -229,9 +275,7 @@
 
         @pl.when(k == 0)
         def _():
-            for copy in coup_out:
-                copy.start()
-            for copy in near_out:
+            for copy in list_out + coup_out + near_first + near_second:
                 copy.start()
 
         for copy in halo_out:
@@ -241,35 +285,57 @@
         def _():
             near_product(k)
 
-        z_all.wait_recv()
-        for copy in y_out:
-            copy.start()
-        for copy in y_out:
-            copy.wait_recv()
-        c_out.start()
-        unpack_table(k, 0)
+        for n in range(len(RUNS)):
+            if z_in[n] is not None:
+                z_in[n].wait_recv()
+            for copy in y_out[n]:
+                copy.start()
 
         @pl.when(k == 0)
         def _():
+            for copy, relay in zip(near_first, near_relay):
+                copy.wait_recv()
+                relay.start()
+            for copy in list_out:
+                copy.wait()
+            for copy in list_in:
+                copy.start()
+
+        for n, run in enumerate(RUNS):
+            for copy in y_out[n]:
+                copy.wait_recv()
+            c_out[n].start()
+            unpack_table(k, 0, run)
+
+        @pl.when(k == 0)
+        def _():
+            for copy in list_in:
+                copy.wait()
             for copy in coup_out:
                 copy.wait()
-            for copy in near_out:
+            for copy in near_first:
+                copy.wait_send()
+            for copy in near_second + near_relay:
                 copy.wait()
             near_product(k)
 
-        c_out.wait()
-        for copy in y_out:
-            copy.wait_send()
+        for n, run in enumerate(RUNS):
+            c_out[n].wait_recv()
+            unpack_table(k, 1, run)
         z_all.wait_send()
-        unpack_table(k, 1)
+        for n in range(len(RUNS)):
+            for copy in y_out[n]:
+                copy.wait_send()
+            c_out[n].wait_send()
 
         for c in range(CL_DEV):
-
-            def fetch(p, carry, c=c):
-                F[c, pl.ds(p * RANK, RANK), :] = U[idx[c * FAR + p]]
-                return carry
-
-            lax.fori_loop(0, FAR, fetch, 0, unroll=8)
+            for s in range(NX):
+
+                def fetch(p, carry, c=c, s=s):
+                    F[c, pl.ds((s * SLOTS + p) * RANK, RANK), :] = U[IX[s, c, p]]
+                    return carry
+
+                lax.fori_loop(0, SLOTS, fetch, 0, unroll=8)
         span = SLOTS * RANK
         for c in range(CL_DEV):
             rows = pl.ds(c * RANK, RANK)
@@ -306,10 +372,10 @@
     grams = GR[...]
     GZ[0] = pack([grams[0:8], grams[8:16]])
     z_out = [
-        to_row(GZ.at[0], GZ.at[d], z_send.at[SB], z_recv.at[SB], z_dev[d]) for d in range(1, NZ)
+        to_row(GZ.at[0], GZ.at[d], z_send.at[SB], z_recv.at[SB, 0], z_dev[d]) for d in range(1, NZ)
     ]
     z_all = to_row(
-        GZ.at[pl.ds(1, NZ - 1)], GZ.at[pl.ds(1, NZ - 1)], z_send.at[SB], z_recv.at[SB], z_dev[1]
+        GZ.at[pl.ds(1, NZ - 1)], GZ.at[pl.ds(1, NZ - 1)], z_send.at[SB], z_recv.at[SB, 0], z_dev[1]
     )
     for copy in z_out:
         copy.start()
@@ -319,7 +385,7 @@
         total = total + GZ[(zz + NZ - src) % NZ]
     GY[0] = total
     y_out = [
-        to_row(GY.at[0], GY.at[d], y_send.at[SB, d - 1], y_recv.at[SB, d - 1], y_dev[d])
+        to_row(GY.at[0], GY.at[d], y_send.at[SB, 0, d - 1], y_recv.at[SB, 0, d - 1], y_dev[d])
         for d in range(1, NY)
     ]
     for copy in y_out:
@@ -330,7 +396,7 @@
     for src in range(1, NY):
         total = total + GY[(yy + NY - src) % NY]
     GC[0] = total
-    c_out = to_row(GC.at[0], GC.at[1], c_send.at[SB], c_recv.at[SB], mate)
+    c_out = to_row(GC.at[0], GC.at[1], c_send.at[SB, 0], c_recv.at[SB, 0], mate)
     c_out.start()
     c_out.wait()
     total = GC[0] + GC[1]
@@ -389,25 +455,17 @@
     live = positions[None, :] < far_count[:, None]
     weighted = jnp.where(live[:, :, None, None], couplings, 0.0)
     weighted = weighted.transpose(0, 2, 1, 3).reshape(CL_DEV * RANK, SLOTS * RANK)
-    own = jnp.concatenate([far_cols, near_cols], axis=1)
-    lists = [own] + [
-        lax.ppermute(own, "col", [(i, (i + s) % NX) for i in range(NX)]) for s in range(1, NX)
-    ]
-    far = jnp.concatenate([piece[:, :SLOTS] for piece in lists], axis=1)
-    near = jnp.concatenate([piece[:, SLOTS:] for piece in lists], axis=1)
-    owner = far // CL_DEV
+    owner = far_cols // CL_DEV
     core, rest = owner % NC, owner // NC
     tile = (
         ((row + NC - core) % NC) * (NY * NZ)
         + ((row // (NC * NZ) + NY - rest // NZ) % NY) * NZ
         + (row // NC + NZ - rest % NZ) % NZ
     )
-    idx = jnp.concatenate(
-        [
-            (tile * CL_DEV + far % CL_DEV).reshape(-1),
-            (near - (row * CL_DEV - REACH)).reshape(-1),
-        ]
+    lists = jnp.concatenate(
+        [tile * CL_DEV + far_cols % CL_DEV, near_cols - (row * CL_DEV - REACH)], axis=1
     ).astype(jnp.int32)
+    lists = jnp.pad(lists, ((0, 8 - CL_DEV), (0, LANES - SLOTS - 1)))
     f32 = jnp.float32
     vmem = pl.BlockSpec(memory_space=pltpu.VMEM)
     dma = pltpu.SemaphoreType.DMA
@@ -417,7 +475,7 @@
             jax.ShapeDtypeStruct((ROWS, LANES), f32),
             jax.ShapeDtypeStruct((24, LANES), f32),
         ),
-        in_specs=[pl.BlockSpec(memory_space=pltpu.SMEM)] + [vmem] * 6,
+        in_specs=[vmem] * 7,
         out_specs=(vmem, vmem),
         scratch_shapes=[
             pltpu.VMEM((SB + 1, ROWS, LANES), f32),
@@ -435,20 +493,23 @@
             pltpu.VMEM((NC, 8, LANES), f32),
             pltpu.VMEM((NX, LANES, LANES), f32),
             pltpu.VMEM((NX, 24, LANES), f32),
-            dma((SB + 1,)), dma((SB + 1,)),
-            dma((SB + 1, NY - 1)), dma((SB + 1, NY - 1)),
-            dma((SB + 1,)), dma((SB + 1,)),
+            pltpu.VMEM((NX - 1, 8, LANES), jnp.int32),
+            pltpu.SMEM((NX, 8, LANES), jnp.int32),
+            dma((SB + 1,)), dma((SB + 1, len(RUNS))),
+            dma((SB + 1, len(RUNS), NY - 1)), dma((SB + 1, len(RUNS), NY - 1)),
+            dma((SB + 1, len(RUNS))), dma((SB + 1, len(RUNS))),
             dma((SB, 2)), dma((SB, 2)),
+            dma((6,)), dma((6,)),
             dma((NX - 1,)), dma((NX - 1,)),
             dma((NX - 1,)), dma((NX - 1,)),
             dma((NX - 1,)), dma((NX - 1,)),
-            dma((NX - 1,)), dma((NX - 1,)),
+            dma((NX - 1,)), dma((NX - 1,)), dma((NX,)),
         ],
         compiler_params=pltpu.CompilerParams(
             collective_id=0, has_side_effects=True, vmem_limit_bytes=48 * 1024 * 1024
         ),
     )(
-        idx,
+        lists,
         residual,
         solution,
         near_field_blocks.reshape(CL_DEV, LEAF_UNKNOWNS, LEAF_UNKNOWNS),

time: 137 us -> 119 us (0.87)
  starting transfers between devices: 10.1 us -> 0 us
  Pallas kernels: 120 us -> 112 us
    ppermute x3 -> x0, starting transfers between devices: 10.1 us -> none  [local(): lax.ppermute(own, 'col', [(i, (i + s) % NX) for i in range(NX)])]
    pallas_call x1, Pallas kernels: 120 us -> 112 us  [local(): pl.pallas_call(kernel, out_shape=(jax.ShapeDtypeStruct((ROWS, LANES), f32...]
    unnamed x17 -> x18, local copies, waits for them, and re-layouts: 2.72 us -> 3.88 us
  transfers between devices with their start and end apart: 3 -> 0, of which waited for: 1 -> 0; matrix products, arithmetic and copies ran while one was open for 1% -> 0% of each run, Pallas kernels for 0% -> 0%
where the time goes in v2:
time: 119 us
  Pallas kernels  112 us (94%)
  local copies, waits for them, and re-layouts  4.82 us (4%)
  other arithmetic  1.24 us (1%)
    pallas_call x1, Pallas kernels, local(): pl.pallas_call(kernel, out_shape=(jax.ShapeDtypeStruct((ROWS, LANES), f32...  112 us
    unnamed x18, local copies, waits for them, and re-layouts  3.88 us

profile of v2, /device:TPU:1, one launch (start us, length us, event | category | flops | bytes accessed | tf_op | source)
XLA Modules:
  0.0 119.0 jit_solution(16903699766600076929)
XLA Ops:
  0.7 0.0 copy-start.6
  0.7 0.6 copy-done.6
  1.3 0.0 copy-start.5
  1.3 0.1 broadcast_compare_fusion
  1.4 0.6 copy-done.5
  2.0 0.0 copy-start.7
  2.0 0.6 copy-done.7
  2.6 0.1 copy.12
  2.7 0.1 pad_add_fusion
  2.8 1.0 select_bitcast_fusion
  3.9 0.0 copy-start.4
  3.9 0.0 copy-start
  3.9 0.1 copy.13
  4.0 0.0 copy-start.1
  4.0 0.0 copy-start.2
  4.0 0.1 reshape.46.coup
  4.2 0.5 copy-done.4
  4.6 0.0 copy-start.3
  4.6 0.1 copy.14
  4.8 0.2 copy-done
  5.0 0.1 copy-done.1
  5.0 0.1 copy-done.2
  5.1 0.4 copy-done.3
  5.5 112.2 %shard_map.104 = (f32[512,128]{1,0:T(8,128)S(1)}, f32[24,128]{1,0:T(8,128)S(1)}) custom-call(s32[8,128]{1,0:T(8,128)S(1)} %pad.4.lists, f32[512,128]{1,0:T(8,128)S(1)} %copy-done.1, f32[512,128]{1,0:T(8,128)S(1)} %copy-done.2, f32[2,256,256]{2,1,0:T(8,128)S(1)} %bitcast.8, f32[32,256]{1,0:T(8,128)S(1)} %reshape.46.coup, f32[2,16,256]{2,1,0:T(8,128)S(1)} %copy-done.3, ...), custom_call_target="tpu_custom_call" | custom-call | tf_op jit(solution)/shard_map/pallas_call | solution.py:472
  117.7 0.6 reshape.47
  118.3 0.7 copy.16
  (4 shorter events, 0.1 us)
Async XLA Ops:
  0.7 0.7 copy-start.6
  1.3 0.7 copy-start.5
  2.0 0.7 copy-start.7
  3.9 0.8 copy-start.4
  3.9 1.1 copy-start
  4.0 1.0 copy-start.1
  4.0 1.1 copy-start.2
  4.6 0.8 copy-start.3

commit v3 on v2

--- a/solution.py
+++ b/solution.py
@@ -29,7 +29,7 @@
 PAIRS = [(a, b) for a in range(SB + 1) for b in range(a, SB + 1)]
 
 
-HIGH = lax.Precision.HIGHEST
+HIGH = lax.Precision.HIGH
 SHIFT = 1.0
 MESH = pl.DeviceIdType.MESH
 
@@ -127,7 +127,7 @@
 
 def kernel(
     lists, res, sol, near, coup, cb, rbt, out, hout,
-    W, T, U, HP, HB, H, F, NB, CP, GR, GZ, GY, GC, XO, XH, IV, IX,
+    W, T, U, HP, HB, H, F, NB, CP, GR, GZ, GY, GC, WF, XH, IV, IX,
     z_send, z_recv, y_send, y_recv, c_send, c_recv, h_send, h_recv,
     n_send, n_recv, p_send, p_recv, o_send, o_recv, q_send, q_recv,
     i_send, i_recv, i_copy,
@@ -172,7 +172,7 @@
         T[k, 0, 0, 0] = pack(pieces)
 
     def stage_halo(k):
-        HP[k] = pack([W[k, pl.ds(q * LANES, LANES), :] for q in range(4)])
+        HP[k, 0] = pack([W[k, pl.ds(q * LANES, LANES), :] for q in range(4)])
 
     stage_table(0)
     stage_halo(0)
@@ -218,6 +218,14 @@
             return carry
 
         lax.fori_loop(run[0], run[1], one, 0)
+
+    def panel_copies(k):
+        return [
+            to_col(
+                HP.at[k, 0], HP.at[k, d], o_send.at[k - 1, d - 1], o_recv.at[k - 1, d - 1], x_dev[d]
+            )
+            for d in range(1, NX)
+        ]
 
     def near_product(k):
         for q in range(4):
@@ -265,8 +273,8 @@
                 )
             )
         halo_out = [
-            to_row(HP.at[k], HB.at[k, 0], h_send.at[k, 0], h_recv.at[k, 0], above),
-            to_row(HP.at[k], HB.at[k, 1], h_send.at[k, 1], h_recv.at[k, 1], below),
+            to_row(HP.at[k, 0], HB.at[k, 0], h_send.at[k, 0], h_recv.at[k, 0], above),
+            to_row(HP.at[k, 0], HB.at[k, 1], h_send.at[k, 1], h_recv.at[k, 1], below),
         ]
         for copy in z_out:
             copy.start()
@@ -283,9 +291,16 @@
 
         @pl.when(k > 0)
         def _():
-            near_product(k)
+            for copy in panel_copies(k):
+                copy.start()
 
         for n in range(len(RUNS)):
+            if n == len(RUNS) - 1:
+
+                @pl.when(k > 0)
+                def _():
+                    near_product(k)
+
             if z_in[n] is not None:
                 z_in[n].wait_recv()
             for copy in y_out[n]:
@@ -379,6 +394,18 @@
     )
     for copy in z_out:
         copy.start()
+    group = lane_group((LANES, LANES))
+    for k in range(1, SB):
+        for copy in panel_copies(k):
+            copy.wait()
+        for q in range(4):
+            full = lanes_to_front(HP[k, col % NX], q)
+            for src in range(1, NX):
+                moved = HP[k, (col + NX - src) % NX]
+                if src != q:
+                    moved = pltpu.roll(moved, ((src - q) * WIDTH) % LANES, 1)
+                full = jnp.where(group == src, moved, full)
+            WF[k - 1, pl.ds(q * LANES, LANES), :] = full
     z_all.wait()
     total = GZ[zz % NZ]
     for src in range(1, NZ):
@@ -405,37 +432,28 @@
     for n, (a, b) in enumerate(PAIRS):
         gram[a][b] = gram[b][a] = total[n : n + 1] if n < 8 else second[n - 8 : n - 7]
     hessen, weights = small_update(gram, 1.0, SB)
-    XH[0] = jnp.zeros((24, LANES), jnp.float32)
     for a in range(SB + 1):
         for b in range(SB):
             XH[0, pl.ds(a * SB + b, 1), :] = hessen[a][b]
-    pieces = []
-    for q in range(4):
-        rows = pl.ds(q * LANES, LANES)
-        value = weights[0] * W[0, rows, :]
-        for k in range(1, SB):
-            value = value + weights[k] * W[k, rows, :]
-        pieces.append(value)
-    XO[0] = pack(pieces)
-    last = []
-    for d in range(1, NX):
-        last.append(to_col(XO.at[0], XO.at[d], o_send.at[d - 1], o_recv.at[d - 1], x_dev[d]))
-        last.append(to_col(XH.at[0], XH.at[d], q_send.at[d - 1], q_recv.at[d - 1], x_dev[d]))
+    for k in range(SB):
+        XH[0, pl.ds((SB + 1) * SB + k, 1), :] = weights[k]
+    last = [
+        to_col(XH.at[0], XH.at[d], q_send.at[d - 1], q_recv.at[d - 1], x_dev[d])
+        for d in range(1, NX)
+    ]
     for copy in last:
         copy.start()
     for copy in last:
         copy.wait()
-    group = lane_group((LANES, LANES))
-    values = [XO[(col + NX - src) % NX] for src in range(NX)]
+    both = pack([XH[(col + NX - src) % NX] for src in range(NX)])
+    hout[...] = both
+    full = [both[(SB + 1) * SB + k : (SB + 1) * SB + k + 1] for k in range(SB)]
     for q in range(4):
         rows = pl.ds(q * LANES, LANES)
-        value = lanes_to_front(values[0], q)
-        for src in range(1, NX):
-            shift = ((src - q) * WIDTH) % LANES
-            moved = pltpu.roll(values[src], shift, 1) if shift else values[src]
-            value = jnp.where(group == src, moved, value)
-        out[rows, :] = sol[rows, :] + value
-    hout[...] = pack([XH[(col + NX - src) % NX] for src in range(NX)])
+        value = sol[rows, :] + full[0] * res[rows, :]
+        for k in range(1, SB):
+            value = value + full[k] * WF[k - 1, rows, :]
+        out[rows, :] = value
 
 
 def local(
@@ -481,7 +499,7 @@
             pltpu.VMEM((SB + 1, ROWS, LANES), f32),
             pltpu.VMEM((SB, NC, NY, NZ, 8, LANES), f32),
             pltpu.VMEM((NROW * CL_DEV, RANK, LANES), f32),
-            pltpu.VMEM((SB, LANES, LANES), f32),
+            pltpu.VMEM((SB, NX, LANES, LANES), f32),
             pltpu.VMEM((SB, 2, LANES, LANES), f32),
             pltpu.VMEM((CL_DEV + 2 * REACH, LEAF_UNKNOWNS, LANES), f32),
             pltpu.VMEM((CL_DEV, FAR * RANK, LANES), f32),
@@ -491,7 +509,7 @@
             pltpu.VMEM((NZ, 8, LANES), f32),
             pltpu.VMEM((NY, 8, LANES), f32),
             pltpu.VMEM((NC, 8, LANES), f32),
-            pltpu.VMEM((NX, LANES, LANES), f32),
+            pltpu.VMEM((SB - 1, ROWS, LANES), f32),
             pltpu.VMEM((NX, 24, LANES), f32),
             pltpu.VMEM((NX - 1, 8, LANES), jnp.int32),
             pltpu.SMEM((NX, 8, LANES), jnp.int32),
@@ -501,7 +519,7 @@
             dma((SB, 2)), dma((SB, 2)),
             dma((6,)), dma((6,)),
             dma((NX - 1,)), dma((NX - 1,)),
-            dma((NX - 1,)), dma((NX - 1,)),
+            dma((SB - 1, NX - 1)), dma((SB - 1, NX - 1)),
             dma((NX - 1,)), dma((NX - 1,)),
             dma((NX - 1,)), dma((NX - 1,)), dma((NX,)),
         ],

time: 119 us -> 109 us (0.916)
  Pallas kernels: 112 us -> 102 us
    pallas_call x1, Pallas kernels: 112 us -> 102 us  [local(): pl.pallas_call(kernel, out_shape=(jax.ShapeDtypeStruct((ROWS, LANES), f32...]
where the time goes in v3:
time: 109 us; the launch traced here: 108 us
  Pallas kernels  102 us (94%)
  local copies, waits for them, and re-layouts  4.82 us (4%)
  other arithmetic  1.24 us (1%)
    pallas_call x1, Pallas kernels, local(): pl.pallas_call(kernel, out_shape=(jax.ShapeDtypeStruct((ROWS, LANES), f32...  102 us
    unnamed x18, local copies, waits for them, and re-layouts  3.88 us

profile of v3, /device:TPU:1, one launch (start us, length us, event | category | flops | bytes accessed | tf_op | source)
XLA Modules:
  0.0 108.5 jit_solution(11547601918704841961)
XLA Ops:
  0.7 0.0 copy-start.6
  0.7 0.6 copy-done.6
  1.3 0.0 copy-start.5
  1.3 0.1 broadcast_compare_fusion
  1.4 0.6 copy-done.5
  2.0 0.0 copy-start.7
  2.0 0.6 copy-done.7
  2.6 0.1 copy.12
  2.7 0.1 pad_add_fusion
  2.8 1.0 select_bitcast_fusion
  3.9 0.0 copy-start.4
  3.9 0.0 copy-start
  3.9 0.1 copy.13
  4.0 0.0 copy-start.1
  4.0 0.0 copy-start.2
  4.0 0.1 reshape.46.coup
  4.2 0.5 copy-done.4
  4.6 0.0 copy-start.3
  4.6 0.1 copy.14
  4.8 0.2 copy-done
  5.0 0.1 copy-done.1
  5.0 0.1 copy-done.2
  5.1 0.4 copy-done.3
  5.5 101.7 %shard_map.104 = (f32[512,128]{1,0:T(8,128)S(1)}, f32[24,128]{1,0:T(8,128)S(1)}) custom-call(s32[8,128]{1,0:T(8,128)S(1)} %pad.4.lists, f32[512,128]{1,0:T(8,128)S(1)} %copy-done.1, f32[512,128]{1,0:T(8,128)S(1)} %copy-done.2, f32[2,256,256]{2,1,0:T(8,128)S(1)} %bitcast.8, f32[32,256]{1,0:T(8,128)S(1)} %reshape.46.coup, f32[2,16,256]{2,1,0:T(8,128)S(1)} %copy-done.3, ...), custom_call_target="tpu_custom_call" | custom-call | tf_op jit(solution)/shard_map/pallas_call | solution.py:490
  107.2 0.6 reshape.47
  107.8 0.7 copy.16
  (4 shorter events, 0.1 us)
Async XLA Ops:
  0.7 0.7 copy-start.6
  1.3 0.7 copy-start.5
  2.0 0.7 copy-start.7
  3.9 0.8 copy-start.4
  3.9 1.1 copy-start
  4.0 1.0 copy-start.1
  4.0 1.1 %copy-start.2 = (f32[512,128]{1,0:T(8,128)S(1)}, f32[512,128]{1,0:T(8,128)}, u32[]{:S(2)}) copy-start(f32[512,128]{1,0:T(8,128)} %sol.1) | copy-start | bytes 786436
  4.6 0.8 copy-start.3

commit v4 on v3

--- a/solution.py
+++ b/solution.py
@@ -176,6 +176,7 @@
 
     stage_table(0)
     stage_halo(0)
+    W[1] = jnp.zeros((ROWS, LANES), jnp.float32)
     pl.semaphore_wait(barrier, (NZ - 1) + (NY - 1) + 3 + (NX - 1))
 
     right, left = x_dev[1], x_dev[NX - 1]
@@ -227,7 +228,7 @@
             for d in range(1, NX)
         ]
 
-    def near_product(k):
+    def near_product(k, more):
         for q in range(4):
             rows = pl.ds((q % 2) * LANES, LANES)
             H[q // 2, rows, :] = lanes_to_front(HB[k, 0], q)
@@ -238,7 +239,8 @@
             total = dot(near[c], H[IX[0, c, SLOTS]])
             for s in range(1, NX):
                 total = total + dot(NB[s - 1, c], H[IX[s, c, SLOTS]])
-            W[k + 1, pl.ds(c * LEAF_UNKNOWNS, LEAF_UNKNOWNS), :] = total
+            rows = pl.ds(c * LEAF_UNKNOWNS, LEAF_UNKNOWNS)
+            W[k + 1, rows, :] = W[k + 1, rows, :] + total if more else total
 
     def step(k, carry):
         z_out = [
@@ -283,7 +285,7 @@
 
         @pl.when(k == 0)
         def _():
-            for copy in list_out + coup_out + near_first + near_second:
+            for copy in near_first + list_out + coup_out + near_second:
                 copy.start()
 
         for copy in halo_out:
@@ -299,7 +301,7 @@
 
                 @pl.when(k > 0)
                 def _():
-                    near_product(k)
+                    near_product(k, False)
 
             if z_in[n] is not None:
                 z_in[n].wait_recv()
@@ -328,11 +330,6 @@
                 copy.wait()
             for copy in coup_out:
                 copy.wait()
-            for copy in near_first:
-                copy.wait_send()
-            for copy in near_second + near_relay:
-                copy.wait()
-            near_product(k)
 
         for n, run in enumerate(RUNS):
             c_out[n].wait_recv()
@@ -358,6 +355,14 @@
             for s in range(1, NX):
                 total = total + dot(CP[s - 1, rows, :], F[c, pl.ds(s * span, span), :])
             W[k + 1, pl.ds(c * LEAF_UNKNOWNS, LEAF_UNKNOWNS), :] += dot(rbt[c], total)
+
+        @pl.when(k == 0)
+        def _():
+            for copy in near_first:
+                copy.wait_send()
+            for copy in near_second + near_relay:
+                copy.wait()
+            near_product(k, True)
 
         @pl.when(k < SB - 1)
         def _():

time: 109 us -> 106 us (0.972)
  Pallas kernels: 102 us -> 99.2 us
    pallas_call x1, Pallas kernels: 102 us -> 99.2 us  [local(): pl.pallas_call(kernel, out_shape=(jax.ShapeDtypeStruct((ROWS, LANES), f32...]
where the time goes in v4:
time: 106 us
  Pallas kernels  99.2 us (94%)
  local copies, waits for them, and re-layouts  4.82 us (5%)
  other arithmetic  1.24 us (1%)
    pallas_call x1, Pallas kernels, local(): pl.pallas_call(kernel, out_shape=(jax.ShapeDtypeStruct((ROWS, LANES), f32...  99.2 us
    unnamed x18, local copies, waits for them, and re-layouts  3.88 us

profile of v4, /device:TPU:1, one launch (start us, length us, event | category | flops | bytes accessed | tf_op | source)
XLA Modules:
  0.0 106.0 jit_solution(7166805723897491639)
XLA Ops:
  0.7 0.0 copy-start.6
  0.7 0.6 copy-done.6
  1.3 0.0 copy-start.5
  1.3 0.1 broadcast_compare_fusion
  1.4 0.6 copy-done.5
  2.0 0.0 copy-start.7
  2.0 0.6 copy-done.7
  2.6 0.1 copy.12
  2.7 0.1 pad_add_fusion
  2.8 1.0 select_bitcast_fusion
  3.9 0.0 copy-start.4
  3.9 0.0 copy-start
  3.9 0.1 copy.13
  4.0 0.0 copy-start.1
  4.0 0.0 copy-start.2
  4.0 0.1 reshape.46.coup
  4.2 0.5 copy-done.4
  4.6 0.0 copy-start.3
  4.6 0.1 copy.14
  4.8 0.2 copy-done
  5.0 0.1 copy-done.1
  5.0 0.1 copy-done.2
  5.1 0.4 copy-done.3
  5.5 99.2 %shard_map.104 = (f32[512,128]{1,0:T(8,128)S(1)}, f32[24,128]{1,0:T(8,128)S(1)}) custom-call(s32[8,128]{1,0:T(8,128)S(1)} %pad.4.lists, f32[512,128]{1,0:T(8,128)S(1)} %copy-done.1, f32[512,128]{1,0:T(8,128)S(1)} %copy-done.2, f32[2,256,256]{2,1,0:T(8,128)S(1)} %bitcast.8, f32[32,256]{1,0:T(8,128)S(1)} %reshape.46.coup, f32[2,16,256]{2,1,0:T(8,128)S(1)} %copy-done.3, ...), custom_call_target="tpu_custom_call" | custom-call | tf_op jit(solution)/shard_map/pallas_call | solution.py:495
  104.7 0.6 reshape.47
  105.3 0.7 copy.16
  (4 shorter events, 0.1 us)
Async XLA Ops:
  0.7 0.7 copy-start.6
  1.3 0.7 copy-start.5
  2.0 0.7 copy-start.7
  3.9 0.8 copy-start.4
  3.9 1.1 copy-start
  4.0 1.0 copy-start.1
  4.0 1.1 %copy-start.2 = (f32[512,128]{1,0:T(8,128)S(1)}, f32[512,128]{1,0:T(8,128)}, u32[]{:S(2)}) copy-start(f32[512,128]{1,0:T(8,128)} %sol.1) | copy-start | bytes 786436
  4.6 0.8 copy-start.3

commit v5 on v4

--- a/solution.py
+++ b/solution.py
@@ -228,17 +228,20 @@
             for d in range(1, NX)
         ]
 
-    def near_product(k, more):
+    def near_panels(k):
         for q in range(4):
             rows = pl.ds((q % 2) * LANES, LANES)
             H[q // 2, rows, :] = lanes_to_front(HB[k, 0], q)
             H[4 + q // 2, rows, :] = lanes_to_front(HB[k, 1], q)
         for c in range(CL_DEV):
             H[2 + c] = W[k, pl.ds(c * LEAF_UNKNOWNS, LEAF_UNKNOWNS), :]
+
+    def near_product(k, more, slots):
         for c in range(CL_DEV):
-            total = dot(near[c], H[IX[0, c, SLOTS]])
-            for s in range(1, NX):
-                total = total + dot(NB[s - 1, c], H[IX[s, c, SLOTS]])
+            total = None
+            for s in slots:
+                term = dot(near[c] if s == 0 else NB[s - 1, c], H[IX[s, c, SLOTS]])
+                total = term if total is None else total + term
             rows = pl.ds(c * LEAF_UNKNOWNS, LEAF_UNKNOWNS)
             W[k + 1, rows, :] = W[k + 1, rows, :] + total if more else total
 
@@ -301,7 +304,8 @@
 
                 @pl.when(k > 0)
                 def _():
-                    near_product(k, False)
+                    near_panels(k)
+                    near_product(k, False, range(NX))
 
             if z_in[n] is not None:
                 z_in[n].wait_recv()
@@ -358,11 +362,15 @@
 
         @pl.when(k == 0)
         def _():
+            near_panels(k)
             for copy in near_first:
                 copy.wait_send()
-            for copy in near_second + near_relay:
+            for copy in near_second:
                 copy.wait()
-            near_product(k, True)
+            near_product(k, True, (0, 1, 3))
+            for copy in near_relay:
+                copy.wait()
+            near_product(k, True, (2,))
 
         @pl.when(k < SB - 1)
         def _():

time: 106 us -> 105 us (level)
  no operation moved by 1% of the time
where the time goes in v5:
time: 105 us
  Pallas kernels  98.3 us (94%)
  local copies, waits for them, and re-layouts  4.82 us (5%)
  other arithmetic  1.24 us (1%)
    pallas_call x1, Pallas kernels, local(): pl.pallas_call(kernel, out_shape=(jax.ShapeDtypeStruct((ROWS, LANES), f32...  98.3 us
    unnamed x18, local copies, waits for them, and re-layouts  3.88 us

profile of v5, /device:TPU:1, one launch (start us, length us, event | category | flops | bytes accessed | tf_op | source)
XLA Modules:
  0.0 105.1 jit_solution(856202061645288750)
XLA Ops:
  0.7 0.0 copy-start.6
  0.7 0.6 copy-done.6
  1.3 0.0 copy-start.5
  1.3 0.1 broadcast_compare_fusion
  1.4 0.6 copy-done.5
  2.0 0.0 copy-start.7
  2.0 0.6 copy-done.7
  2.6 0.1 copy.12
  2.7 0.1 pad_add_fusion
  2.8 1.0 select_bitcast_fusion
  3.9 0.0 copy-start.4
  3.9 0.0 copy-start
  3.9 0.1 copy.13
  4.0 0.0 copy-start.1
  4.0 0.0 copy-start.2
  4.0 0.1 reshape.46.coup
  4.2 0.5 copy-done.4
  4.6 0.0 copy-start.3
  4.6 0.1 copy.14
  4.8 0.2 copy-done
  5.0 0.1 copy-done.1
  5.0 0.1 copy-done.2
  5.1 0.4 copy-done.3
  5.5 98.3 %shard_map.104 = (f32[512,128]{1,0:T(8,128)S(1)}, f32[24,128]{1,0:T(8,128)S(1)}) custom-call(s32[8,128]{1,0:T(8,128)S(1)} %pad.4.lists, f32[512,128]{1,0:T(8,128)S(1)} %copy-done.1, f32[512,128]{1,0:T(8,128)S(1)} %copy-done.2, f32[2,256,256]{2,1,0:T(8,128)S(1)} %bitcast.8, f32[32,256]{1,0:T(8,128)S(1)} %reshape.46.coup, f32[2,16,256]{2,1,0:T(8,128)S(1)} %copy-done.3, ...), custom_call_target="tpu_custom_call" | custom-call | tf_op jit(solution)/shard_map/pallas_call | solution.py:503
  103.8 0.6 reshape.47
  104.4 0.7 copy.16
  (4 shorter events, 0.1 us)
Async XLA Ops:
  0.7 0.7 copy-start.6
  1.3 0.7 copy-start.5
  2.0 0.7 copy-start.7
  3.9 0.8 copy-start.4
  3.9 1.1 %copy-start = (f32[2,1,256,256]{3,2,1,0:T(8,128)S(1)}, f32[2,1,256,256]{3,2,1,0:T(8,128)}, u32[]{:S(2)}) copy-start(f32[2,1,256,256]{3,2,1,0:T(8,128)} %param.11) | copy-start | bytes 1572868
  4.0 1.0 copy-start.1
  4.0 1.1 %copy-start.2 = (f32[512,128]{1,0:T(8,128)S(1)}, f32[512,128]{1,0:T(8,128)}, u32[]{:S(2)}) copy-start(f32[512,128]{1,0:T(8,128)} %sol.1) | copy-start | bytes 786436
  4.6 0.8 copy-start.3
